TPU v7x, 32 devices: a whole 2x2x4 slice. The times are simulated.
32 devices in a mesh: row: 2 (over y), col: 16 (over z, x, core).
Axes of the slice: x: 2, y: 2, z: 4, core: 2. Of those that a mesh axis runs over, the one named last changes fastest.
Arguments:
- queries: bfloat16 [8192, 1024], P(('row', 'col')), may hold values from -8 to 8
- key_rows: bfloat16 [8192, 1024], P(('row', 'col')), may hold values from -8 to 8
- value_rows: bfloat16 [8192, 1024], P(('row', 'col')), may hold values from -6 to 6
- out_grad: bfloat16 [8192, 1024], P(('row', 'col')), may hold values from -6 to 6
- dropout_bits: int32 [8192, 128], P(('row', 'col')), may hold values from 0 to 255, as said below
- partner: int32 [3, 2, 16], replicated, may hold values from 0 to 15, each once within a row
- block_pick: int32 [3, 2, 16], replicated, may hold values from 0 to 1
- global_blocks: int32 [2], replicated, may hold values from 0 to 63
Outputs:
- attended: bfloat16 [8192, 1024], P(('row', 'col'))
- query_grad: bfloat16 [8192, 1024], P(('row', 'col'))
- key_grad: bfloat16 [8192, 1024], P(('row', 'col'))
- value_grad: bfloat16 [8192, 1024], P(('row', 'col'))
Inputs may be any that keep to these rules, and one draw needn't show every extreme that they name: `dropout_bits`: each word packs 8 flags of 0 or 1 in its low bits. partner[r, a, :] is a permutation of the places 0 to 15.
All inputs are finite; a program needn't handle non-finite values.
Results may differ from a plain program's by a relative error of at most 0.0085.
Values may be sent and summed in bfloat16 or wider, within the bound.
A program may use at most 128 MiB of HBM per device.

v0:
```python
import jax
import jax.numpy as jnp
from jax import lax
from jax.sharding import PartitionSpec as P

HEADS = 16
HEAD_DIM = 64
BLOCK = 128
NGLOBAL = 2
NMATCH = 3
score_scale = 0.125
keep_scale = 1.0 / 0.9


def extended_2(value, sides, width):
    for axis, dim in sides:
        size, length = (lax.axis_size(axis), value.shape[dim])
        up = [(i, (i + 1) % size) for i in range(size)]
        down = [(j, i) for i, j in up]
        last = lax.slice_in_dim(value, length - width, length, axis=dim)
        leading = lax.slice_in_dim(value, 0, width, axis=dim)
        before = lax.ppermute(last, axis, up)
        after = lax.ppermute(leading, axis, down)
        value = jnp.concatenate([before, value, after], axis=dim)
    return value


def spread(value, axis, root):
    mine = lax.axis_index(axis) == root
    return lax.psum(jnp.where(mine, value, jnp.zeros_like(value)), axis)


def unpack_bits(packed):
    shifts = jnp.arange(8, dtype=jnp.int32)
    flags = jnp.right_shift(packed[..., None], shifts) & 1
    return flags.reshape(packed.shape[:-1] + (packed.shape[-1] * 8,))


def split_heads(array, lower, upper, group_heads):
    part_cols = array[..., lower:upper]
    return part_cols.reshape(
        part_cols.shape[:-1] + (group_heads, part_cols.shape[-1] // group_heads)
    )


def route_blocks(pieces_in, ordering):
    total_cols = lax.axis_size("col")
    matched, rows_in, channels = pieces_in.shape
    split_rows = pieces_in.reshape(matched, total_cols, rows_in // total_cols, channels)
    spread_out = lax.all_to_all(split_rows, "col", split_axis=1, concat_axis=1, tiled=True)
    arranged = jnp.stack([spread_out[matching][ordering[matching]] for matching in range(matched)])
    arrived = lax.all_to_all(arranged, "col", split_axis=1, concat_axis=1, tiled=True)
    return arrived.reshape(matched, rows_in, channels)


def route_all(pieces_in, ordering):
    return route_blocks(pieces_in, ordering)


def body(queries, key_rows, value_rows, out_grad, dropout_bits, partner, block_pick, global_blocks):
    tokens_here, model_width = queries.shape
    blocks_here = tokens_here // BLOCK
    group_heads = min(4, HEADS)
    group_width = group_heads * HEAD_DIM
    near_rows = 3 * BLOCK
    both_rows = jnp.concatenate([key_rows, value_rows], 1)
    band_index = lax.axis_index("row")
    place_index = lax.axis_index("col")
    total_cols = lax.axis_size("col")
    segment = band_index * total_cols + place_index
    extended = extended_2(both_rows, ((("row", "col"), 0),), BLOCK)
    shared_parts = []
    for global_slot in range(NGLOBAL):
        position = global_blocks[global_slot]
        source_piece = lax.dynamic_slice_in_dim(both_rows, position % blocks_here * BLOCK, BLOCK, 0)
        shared_parts.append(spread(source_piece, ("row", "col"), position // blocks_here))
    ordering = lax.dynamic_index_in_dim(partner, band_index, 1, keepdims=False)
    picks_row = lax.dynamic_index_in_dim(block_pick, band_index, 1, keepdims=False)
    col_ids = jnp.arange(total_cols, dtype=jnp.int32)
    inverse = jnp.sum(
        jnp.where(ordering[:, :, None] == col_ids[None, None, :], col_ids[None, :, None], 0), axis=1
    )
    askers = lax.dynamic_index_in_dim(inverse, place_index, 1, keepdims=False)
    wanted = jnp.take_along_axis(picks_row, askers[:, None], axis=1)[:, 0]
    outgoing = jnp.stack(
        [
            lax.dynamic_slice_in_dim(both_rows, wanted[matching] * BLOCK, BLOCK, 0)
            for matching in range(NMATCH)
        ]
    )
    fetched = route_all(outgoing, ordering)
    shared = jnp.concatenate(shared_parts + [fetched.reshape(NMATCH * BLOCK, 2 * model_width)], 0)
    windows = jnp.stack(
        [
            extended[start_block * BLOCK : start_block * BLOCK + near_rows]
            for start_block in range(blocks_here)
        ]
    )
    keep_mask = (unpack_bits(dropout_bits).astype(jnp.float32) * keep_scale).reshape(
        blocks_here, BLOCK, -1
    )
    keep_near = keep_mask[..., :near_rows][:, None]
    keep_far = keep_mask[..., near_rows:][:, None]
    query_blocks = queries.reshape(blocks_here, BLOCK, model_width)
    grad_blocks = out_grad.reshape(blocks_here, BLOCK, model_width)
    out_parts, query_parts = ([], [])
    key_near_parts, value_near_parts, key_far_parts, value_far_parts = ([], [], [], [])
    for group_index in range(HEADS // group_heads):
        lower = group_index * group_width
        upper = lower + group_width
        query_group = split_heads(query_blocks, lower, upper, group_heads)
        grad_group = split_heads(grad_blocks, lower, upper, group_heads)
        keys_near = split_heads(windows, lower, upper, group_heads)
        values_near = split_heads(windows, model_width + lower, model_width + upper, group_heads)
        keys_far = split_heads(shared, lower, upper, group_heads)
        values_far = split_heads(shared, model_width + lower, model_width + upper, group_heads)
        score_near = (
            jnp.einsum(
                "jqgd,jkgd->jgqk", query_group, keys_near, preferred_element_type=jnp.float32
            )
            * score_scale
        )
        score_far = (
            jnp.einsum("jqgd,kgd->jgqk", query_group, keys_far, preferred_element_type=jnp.float32)
            * score_scale
        )
        top = jnp.maximum(
            jnp.max(score_near, -1, keepdims=True), jnp.max(score_far, -1, keepdims=True)
        )
        total = jnp.sum(jnp.exp(score_near - top), -1, keepdims=True) + jnp.sum(
            jnp.exp(score_far - top), -1, keepdims=True
        )
        log_total = top + jnp.log(total)
        probs_near = jnp.exp(score_near - log_total)
        probs_far = jnp.exp(score_far - log_total)
        dropped_near = (probs_near * keep_near).astype(jnp.bfloat16)
        dropped_far = (probs_far * keep_far).astype(jnp.bfloat16)
        output_group = jnp.einsum(
            "jgqk,jkgd->jqgd", dropped_near, values_near, preferred_element_type=jnp.float32
        ) + jnp.einsum(
            "jgqk,kgd->jqgd", dropped_far, values_far, preferred_element_type=jnp.float32
        )
        out_parts.append(output_group.reshape(blocks_here, BLOCK, group_width))
        grad_near = (
            jnp.einsum(
                "jqgd,jkgd->jgqk", grad_group, values_near, preferred_element_type=jnp.float32
            )
            * keep_near
        )
        grad_far = (
            jnp.einsum("jqgd,kgd->jgqk", grad_group, values_far, preferred_element_type=jnp.float32)
            * keep_far
        )
        delta = jnp.sum(probs_near * grad_near, -1, keepdims=True) + jnp.sum(
            probs_far * grad_far, -1, keepdims=True
        )
        dscore_near = (probs_near * (grad_near - delta)).astype(jnp.bfloat16)
        dscore_far = (probs_far * (grad_far - delta)).astype(jnp.bfloat16)
        query_group_grad = score_scale * (
            jnp.einsum(
                "jgqk,jkgd->jqgd", dscore_near, keys_near, preferred_element_type=jnp.float32
            )
            + jnp.einsum("jgqk,kgd->jqgd", dscore_far, keys_far, preferred_element_type=jnp.float32)
        )
        query_parts.append(query_group_grad.reshape(blocks_here, BLOCK, group_width))
        key_near_parts.append(
            (
                score_scale
                * jnp.einsum(
                    "jgqk,jqgd->jkgd", dscore_near, query_group, preferred_element_type=jnp.float32
                )
            ).reshape(blocks_here, near_rows, group_width)
        )
        value_near_parts.append(
            jnp.einsum(
                "jgqk,jqgd->jkgd", dropped_near, grad_group, preferred_element_type=jnp.float32
            ).reshape(blocks_here, near_rows, group_width)
        )
        key_far_parts.append(
            (
                score_scale
                * jnp.einsum(
                    "jgqk,jqgd->kgd", dscore_far, query_group, preferred_element_type=jnp.float32
                )
            ).reshape(-1, group_width)
        )
        value_far_parts.append(
            jnp.einsum(
                "jgqk,jqgd->kgd", dropped_far, grad_group, preferred_element_type=jnp.float32
            ).reshape(-1, group_width)
        )
    attended = jnp.concatenate(out_parts, -1).astype(jnp.bfloat16).reshape(tokens_here, model_width)
    query_grad = (
        jnp.concatenate(query_parts, -1).astype(jnp.bfloat16).reshape(tokens_here, model_width)
    )
    near_grads = jnp.concatenate(key_near_parts + value_near_parts, -1)
    far_grads = jnp.concatenate(key_far_parts + value_far_parts, -1)
    window_total = jnp.zeros((tokens_here + 2 * BLOCK, 2 * model_width), jnp.float32)
    for start_block in range(blocks_here):
        window_total = window_total.at[start_block * BLOCK : start_block * BLOCK + near_rows].add(
            near_grads[start_block]
        )
    rims = jnp.concatenate([window_total[:BLOCK], window_total[-BLOCK:]], 0).astype(jnp.bfloat16)
    returned = extended_2(rims, ((("row", "col"), 0),), BLOCK)
    gradients = window_total[BLOCK : BLOCK + tokens_here]
    gradients = gradients.at[:BLOCK].add(returned[:BLOCK].astype(jnp.float32))
    gradients = gradients.at[tokens_here - BLOCK :].add(returned[3 * BLOCK :].astype(jnp.float32))
    global_sum = lax.psum(far_grads[: NGLOBAL * BLOCK], ("row", "col"))
    for global_slot in range(NGLOBAL):
        position = global_blocks[global_slot]
        owner_here = position // blocks_here == segment
        row_offset = position % blocks_here * BLOCK
        current = lax.dynamic_slice_in_dim(gradients, row_offset, BLOCK, 0)
        addition = jnp.where(
            owner_here, global_sum[global_slot * BLOCK : (global_slot + 1) * BLOCK], 0.0
        )
        gradients = lax.dynamic_update_slice_in_dim(gradients, current + addition, row_offset, 0)
    random_grads = (
        far_grads[NGLOBAL * BLOCK :].reshape(NMATCH, BLOCK, 2 * model_width).astype(jnp.bfloat16)
    )
    came_back = route_all(random_grads, inverse)
    for matching in range(NMATCH):
        row_offset = wanted[matching] * BLOCK
        current = lax.dynamic_slice_in_dim(gradients, row_offset, BLOCK, 0)
        gradients = lax.dynamic_update_slice_in_dim(
            gradients, current + came_back[matching].astype(jnp.float32), row_offset, 0
        )
    return (
        attended,
        query_grad,
        gradients[:, :model_width].astype(jnp.bfloat16),
        gradients[:, model_width:].astype(jnp.bfloat16),
    )


def solution(mesh):
    in_specs = (
        P(("row", "col"), None),
        P(("row", "col"), None),
        P(("row", "col"), None),
        P(("row", "col"), None),
        P(("row", "col"), None),
        P(),
        P(),
        P(),
    )
    out_specs = (
        P(("row", "col"), None),
        P(("row", "col"), None),
        P(("row", "col"), None),
        P(("row", "col"), None),
    )
    return jax.shard_map(body, mesh=mesh, in_specs=in_specs, out_specs=out_specs, check_vma=False)
```

profile of v0, /device:TPU:0, one launch (start us, length us, event | category | flops | bytes accessed | tf_op | source)
XLA Modules:
  0.0 565.9 jit_solution(7647314221902579277)
XLA Ops:
  22.5 7.5 %all-to-all-start = ((bf16[3,16,8,2048]{3,2,0,1:T(8,128)(2,1)}), bf16[3,16,8,2048]{3,2,0,1:T(8,128)(2,1)S(1)}, u32[]{:S(2)}, u32[]{:S(2)}) async-start(bf16[3,16,8,2048]{3,2,0,1:T(8,128)(2,1)} %pad_maximum_fusion.1), calls=%async_computation | async-start | bytes 3145728 | tf_op jit(solution)/shard_map/all_to_all | solution.py:50
  30.1 31.8 %all-to-all-done = bf16[3,16,8,2048]{3,2,0,1:T(8,128)(2,1)S(1)} async-done(((bf16[3,16,8,2048]{3,2,0,1:T(8,128)(2,1)}), bf16[3,16,8,2048]{3,2,0,1:T(8,128)(2,1)S(1)}, u32[]{:S(2)}, u32[]{:S(2)}) %all-to-all-start) | async-done | bytes 1572896 | tf_op jit(solution)/shard_map/all_to_all | solution.py:50
  68.3 9.3 %all-to-all-start.1 = ((bf16[3,16,8,2048]{3,2,0,1:T(8,128)(2,1)}), bf16[3,16,8,2048]{3,2,0,1:T(8,128)(2,1)}, u32[]{:S(2)}, u32[]{:S(2)}) async-start(bf16[3,16,8,2048]{3,2,0,1:T(8,128)(2,1)} %copy.750), calls=%async_computation.1 | async-start | bytes 3145728 | tf_op jit(solution)/shard_map/all_to_all | solution.py:52
  78.1 5.0 collective-permute-start.1
  83.9 3.5 convert_multiply_fusion
  95.9 23.3 %collective-permute-done = bf16[128,2048]{1,0:T(8,128)(2,1)} collective-permute-done((bf16[128,2048]{1,0:T(8,128)(2,1)}, bf16[128,2048]{1,0:T(8,128)(2,1)}, u32[]{:S(2)}, u32[]{:S(2)}) %collective-permute-start) | collective-permute-done | bytes 524320 | tf_op jit(solution)/shard_map/ppermute | solution.py:22
  132.9 2.7 copy.751
  135.7 93.7 %all-reduce.7.cloned.1.call-done = (bf16[128,2048]{1,0:T(8,128)(2,1)}, bf16[128,2048]{1,0:T(8,128)(2,1)}) async-done(((bf16[128,2048]{1,0:T(8,128)(2,1)}, bf16[128,2048]{1,0:T(8,128)(2,1)}), (bf16[128,2048]{1,0:T(8,128)(2,1)}, bf16[128,2048]{1,0:T(8,128)(2,1)})) %all-reduce.7.cloned.1.call-update) | async-done | bytes 1048592 | tf_op jit(solution)/shard_map/psum | solution.py:30
  272.3 3.9 multiply_reduce_fusion.3
  278.0 7.7 %multiply_convert_fusion.3 = (bf16[2,4,128,640]{2,3,0,1:T(8,128)(2,1)}, bf16[2,4,128,640]{2,3,0,1:T(8,128)(2,1)}, bf16[2,4,128,640]{2,3,0,1:T(8,128)(2,1)}, bf16...) fusion(f32[4,640,2,128]{3,1,2,0:T(8,128)} %get-tuple-element.16, ...), kind=kLoop, calls=%fused_computation.61 | loop fusion | flops 20971520 | bytes 32145408 | tf_op jit(solution)/shard_map/convert_element_type | solution.py:158
  285.8 2.7 fusion.41
  290.7 2.7 fusion.42
  295.5 2.7 fusion.43
  300.4 2.7 fusion.44
  305.2 2.7 fusion.118
  310.0 2.6 fusion.114
  314.8 2.7 fusion.110
  319.6 2.7 fusion.106
  378.4 4.7 all-to-all-start.2
  397.9 21.7 %all-to-all-done.2 = bf16[3,16,8,2048]{3,2,0,1:T(8,128)(2,1)} async-done(((bf16[3,16,8,2048]{3,2,0,1:T(8,128)(2,1)}), bf16[3,16,8,2048]{3,2,0,1:T(8,128)(2,1)}, u32[]{:S(2)}, u32[]{:S(2)}) %all-to-all-start.2) | async-done | bytes 1572896 | tf_op jit(solution)/shard_map/all_to_all | solution.py:50
  432.5 13.6 %all-to-all-start.3 = ((bf16[3,16,8,2048]{3,2,0,1:T(8,128)(2,1)}), bf16[3,16,8,2048]{3,2,0,1:T(8,128)(2,1)}, u32[]{:S(2)}, u32[]{:S(2)}) async-start(bf16[3,16,8,2048]{3,2,0,1:T(8,128)(2,1)} %copy.873), calls=%async_computation.3 | async-start | bytes 3145728 | tf_op jit(solution)/shard_map/all_to_all | solution.py:52
  452.5 4.6 collective-permute-start.3
  459.5 24.8 %collective-permute-done.2 = bf16[128,2048]{1,0:T(8,128)(2,1)} collective-permute-done((bf16[128,2048]{1,0:T(8,128)(2,1)}, bf16[128,2048]{1,0:T(8,128)(2,1)}, u32[]{:S(2)}, u32[]{:S(2)}) %collective-permute-start.2) | collective-permute-done | bytes 524320 | tf_op jit(solution)/shard_map/ppermute | solution.py:22
  487.1 64.7 %all-reduce.5.cloned.1.call-done = f32[256,2048]{1,0:T(8,128)} async-done(((f32[256,2048]{1,0:T(8,128)}), f32[256,2048]{1,0:T(8,128)}) %all-reduce.5.cloned.1.call-update) | async-done | bytes 2097168 | tf_op jit(solution)/shard_map/psum | solution.py:208
  (445 shorter events, 198.8 us)
Async XLA Ops:
  7.2 12.4 %copy-start.84 = (bf16[256,1024]{1,0:T(8,128)(2,1)S(1)}, bf16[256,1024]{1,0:T(8,128)(2,1)}, u32[]{:S(2)}) copy-start(bf16[256,1024]{1,0:T(8,128)(2,1)} %param.18) | copy-start | bytes 1572868
  22.5 39.4 %all-to-all-start = ((bf16[3,16,8,2048]{3,2,0,1:T(8,128)(2,1)}), bf16[3,16,8,2048]{3,2,0,1:T(8,128)(2,1)S(1)}, u32[]{:S(2)}, u32[]{:S(2)}) async-start(bf16[3,16,8,2048]{3,2,0,1:T(8,128)(2,1)} %pad_maximum_fusion.1), calls=%async_computation | async-start | bytes 3145728 | tf_op jit(solution)/shard_map/all_to_all | solution.py:50
  68.3 14.9 %copy-start.95 = (s32[256,128]{1,0:T(8,128)S(1)}, s32[256,128]{1,0:T(8,128)}, u32[]{:S(2)}) copy-start(s32[256,128]{1,0:T(8,128)} %param.20) | copy-start | bytes 393220
  68.3 64.6 %all-to-all-start.1 = ((bf16[3,16,8,2048]{3,2,0,1:T(8,128)(2,1)}), bf16[3,16,8,2048]{3,2,0,1:T(8,128)(2,1)}, u32[]{:S(2)}, u32[]{:S(2)}) async-start(bf16[3,16,8,2048]{3,2,0,1:T(8,128)(2,1)} %copy.750), calls=%async_computation.1 | async-start | bytes 3145728 | tf_op jit(solution)/shard_map/all_to_all | solution.py:52
  77.6 151.8 %all-reduce.7.cloned.1.call-start = ((), (), s32[]{:S(2)}) async-start(), calls=%async_computation.5 | async-start | bytes 2097152 | tf_op jit(solution)/shard_map/psum | solution.py:30
  77.7 41.5 %collective-permute-start = (bf16[128,2048]{1,0:T(8,128)(2,1)}, bf16[128,2048]{1,0:T(8,128)(2,1)}, u32[]{:S(2)}, u32[]{:S(2)}) collective-permute-start(bf16[128,2048]{1,0:T(8,128)(2,1)} %get-tuple-element.116), channel_id=1, source_target_pairs={{0,1},{1,2},{2,3},{3,4},{4,5},{5,6},{6,7},{7,8},{8,9},{9,10},{10,1... | collective-permute-start | bytes 1572872 | tf_op jit(solution)/shard_map/ppermute | solution.py:22
  78.1 41.1 %collective-permute-start.1 = (bf16[128,2048]{1,0:T(8,128)(2,1)}, bf16[128,2048]{1,0:T(8,128)(2,1)}, u32[]{:S(2)}, u32[]{:S(2)}) collective-permute-start(bf16[128,2048]{1,0:T(8,128)(2,1)} %get-tuple-element.122), channel_id=1, source_target_pairs={{1,0},{2,1},{3,2},{4,3},{5,4},{6,5},{7,6},{8,7},{9,8},{10,9},{11,1... | collective-permute-start | bytes 1572872 | tf_op jit(solution)/shard_map/ppermute | solution.py:23
  89.9 39.3 %copy-start.50 = (bf16[2,128,256]{1,2,0:T(8,128)(2,1)}, bf16[2,128,256]{1,2,0:T(8,128)(2,1)S(1)}, u32[]{:S(2)}) copy-start(bf16[2,128,256]{1,2,0:T(8,128)(2,1)S(1)} %copy.941) | copy-start | bytes 393220
  90.0 40.9 %copy-start.48 = (bf16[2,128,256]{1,2,0:T(8,128)(2,1)}, bf16[2,128,256]{1,2,0:T(8,128)(2,1)S(1)}, u32[]{:S(2)}) copy-start(bf16[2,128,256]{1,2,0:T(8,128)(2,1)S(1)} %copy.940) | copy-start | bytes 393220
  90.2 38.0 %copy-start.42 = (bf16[2,128,256]{1,2,0:T(8,128)(2,1)}, bf16[2,128,256]{1,2,0:T(8,128)(2,1)S(1)}, u32[]{:S(2)}) copy-start(bf16[2,128,256]{1,2,0:T(8,128)(2,1)S(1)} %copy.942) | copy-start | bytes 393220
  276.2 9.6 %copy-start.96 = (f32[2,4,128]{2,1,0:T(4,128)}, f32[2,4,128]{2,1,0:T(4,128)S(1)}, u32[]{:S(2)}) copy-start(f32[2,4,128]{2,1,0:T(4,128)S(1)} %copy_add_fusion) | copy-start | bytes 12292
  276.8 8.9 %copy-start.98 = (f32[2,4,128]{2,1,0:T(4,128)}, f32[2,4,128]{2,1,0:T(4,128)S(1)}, u32[]{:S(2)}) copy-start(f32[2,4,128]{2,1,0:T(4,128)S(1)} %copy_add_fusion.2) | copy-start | bytes 12292
  378.4 41.2 %all-to-all-start.2 = ((bf16[3,16,8,2048]{3,2,0,1:T(8,128)(2,1)}), bf16[3,16,8,2048]{3,2,0,1:T(8,128)(2,1)}, u32[]{:S(2)}, u32[]{:S(2)}) async-start(bf16[3,16,8,2048]{3,2,0,1:T(8,128)(2,1)} %copy.872), calls=%async_computation.2 | async-start | bytes 3145728 | tf_op jit(solution)/shard_map/all_to_all | solution.py:50
  383.1 168.6 %all-reduce.5.cloned.1.call-start = ((), (), s32[]{:S(2)}) async-start(), calls=%async_computation.4 | async-start | bytes 4194304 | tf_op jit(solution)/shard_map/psum | solution.py:208
  432.5 121.4 %all-to-all-start.3 = ((bf16[3,16,8,2048]{3,2,0,1:T(8,128)(2,1)}), bf16[3,16,8,2048]{3,2,0,1:T(8,128)(2,1)}, u32[]{:S(2)}, u32[]{:S(2)}) async-start(bf16[3,16,8,2048]{3,2,0,1:T(8,128)(2,1)} %copy.873), calls=%async_computation.3 | async-start | bytes 3145728 | tf_op jit(solution)/shard_map/all_to_all | solution.py:52
  448.6 8.6 %copy-start.6 = (f32[384,2048]{1,0:T(8,128)}, f32[384,2048]{1,0:T(8,128)S(1)}, u32[]{:S(2)}) copy-start(f32[384,2048]{1,0:T(8,128)S(1)} %fusion) | copy-start | bytes 9437188
  448.6 8.4 %copy-start.88 = (bf16[32,8,2,128]{3,1,2,0:T(8,128)(2,1)S(1)}, bf16[32,8,2,128]{3,1,2,0:T(8,128)(2,1)}, u32[]{:S(2)}) copy-start(bf16[32,8,2,128]{3,1,2,0:T(8,128)(2,1)} %copy.1074) | copy-start | bytes 393220
  448.7 8.4 %copy-start.89 = (bf16[32,8,2,128]{3,1,2,0:T(8,128)(2,1)S(1)}, bf16[32,8,2,128]{3,1,2,0:T(8,128)(2,1)}, u32[]{:S(2)}) copy-start(bf16[32,8,2,128]{3,1,2,0:T(8,128)(2,1)} %copy.1073) | copy-start | bytes 393220
  448.7 8.5 %copy-start.87 = (bf16[32,8,2,128]{3,1,2,0:T(8,128)(2,1)S(1)}, bf16[32,8,2,128]{3,1,2,0:T(8,128)(2,1)}, u32[]{:S(2)}) copy-start(bf16[32,8,2,128]{3,1,2,0:T(8,128)(2,1)} %copy.1070) | copy-start | bytes 393220
  448.7 8.5 %copy-start.90 = (bf16[32,8,2,128]{3,1,2,0:T(8,128)(2,1)S(1)}, bf16[32,8,2,128]{3,1,2,0:T(8,128)(2,1)}, u32[]{:S(2)}) copy-start(bf16[32,8,2,128]{3,1,2,0:T(8,128)(2,1)} %copy.1069) | copy-start | bytes 393220
  448.7 8.5 %copy-start.92 = (bf16[32,8,2,128]{3,1,2,0:T(8,128)(2,1)S(1)}, bf16[32,8,2,128]{3,1,2,0:T(8,128)(2,1)}, u32[]{:S(2)}) copy-start(bf16[32,8,2,128]{3,1,2,0:T(8,128)(2,1)} %copy.1068) | copy-start | bytes 393220
  448.7 8.5 %copy-start.94 = (bf16[32,8,2,128]{3,1,2,0:T(8,128)(2,1)S(1)}, bf16[32,8,2,128]{3,1,2,0:T(8,128)(2,1)}, u32[]{:S(2)}) copy-start(bf16[32,8,2,128]{3,1,2,0:T(8,128)(2,1)} %copy.1067) | copy-start | bytes 393220
  449.6 34.7 %collective-permute-start.2 = (bf16[128,2048]{1,0:T(8,128)(2,1)}, bf16[128,2048]{1,0:T(8,128)(2,1)}, u32[]{:S(2)}, u32[]{:S(2)}) collective-permute-start(bf16[128,2048]{1,0:T(8,128)(2,1)} %slice.505), channel_id=1, source_target_pairs={{0,1},{1,2},{2,3},{3,4},{4,5},{5,6},{6,7},{7,8},{8,9},{9,10},{10,1... | collective-permute-start | bytes 1572872 | tf_op jit(solution)/shard_map/ppermute | solution.py:22
  452.5 33.3 %collective-permute-start.3 = (bf16[128,2048]{1,0:T(8,128)(2,1)}, bf16[128,2048]{1,0:T(8,128)(2,1)}, u32[]{:S(2)}, u32[]{:S(2)}) collective-permute-start(bf16[128,2048]{1,0:T(8,128)(2,1)} %fusion.98), channel_id=1, source_target_pairs={{1,0},{2,1},{3,2},{4,3},{5,4},{6,5},{7,6},{8,7},{9,8},{10,9},{11,1... | collective-permute-start | bytes 1572872 | tf_op jit(solution)/shard_map/ppermute | solution.py:23
  (93 other events, 201.3 us)
Sparse Core Ops, SparseCore 0:
  84.4 144.9 all-reduce.6
  391.0 160.7 all-reduce.4
where the time goes:
time: 572 us; the launch traced here: 566 us
  waiting for transfers between devices  260 us (45%)
  local copies, waits for them, and re-layouts  133 us (23%)
  matrix products  64.1 us (11%)
  starting transfers between devices  45.6 us (8%)
  other arithmetic  39.9 us (7%)
  between operations  23.1 us (4%)
    psum x1, waiting for transfers between devices, spread(): return lax.psum(jnp.where(mine, value, jnp.zeros_like(value)), axis)  93.7 us
    psum x1, waiting for transfers between devices, body(): global_sum = lax.psum(far_grads[:NGLOBAL * BLOCK], ('row', 'col'))  64.7 us
    all_to_all x2, waiting for transfers between devices, route_blocks(): lax.all_to_all(split_rows, 'col', split_axis=1, concat_axis=1, tiled=True)  53.5 us
    ppermute x2, waiting for transfers between devices, extended_2(): before = lax.ppermute(last, axis, up)  48.1 us
    unnamed x249, local copies, waits for them, and re-layouts  35.2 us
    all_to_all x2, starting transfers between devices, route_blocks(): lax.all_to_all(arranged, 'col', split_axis=1, concat_axis=1, tiled=True)  22.9 us
    slice x19, local copies, waits for them, and re-layouts, split_heads(): part_cols = array[..., lower:upper]  22.8 us
    all_to_all x2, starting transfers between devices, route_blocks(): lax.all_to_all(split_rows, 'col', split_axis=1, concat_axis=1, tiled=True)  12.3 us
  transfers between devices with their start and end apart: 10, of which 6 were waited for; matrix products, arithmetic and copies ran while one was open for 11% of the time, Pallas kernels for 0%

commit v1 on v0

--- a/solution.py
+++ b/solution.py
@@ -205,7 +205,7 @@
     gradients = window_total[BLOCK : BLOCK + tokens_here]
     gradients = gradients.at[:BLOCK].add(returned[:BLOCK].astype(jnp.float32))
     gradients = gradients.at[tokens_here - BLOCK :].add(returned[3 * BLOCK :].astype(jnp.float32))
-    global_sum = lax.psum(far_grads[: NGLOBAL * BLOCK], ("row", "col"))
+    global_sum = jnp.sum(lax.all_gather(far_grads[: NGLOBAL * BLOCK], ("row", "col")), axis=0)
     for global_slot in range(NGLOBAL):
         position = global_blocks[global_slot]
         owner_here = position // blocks_here == segment

time: 572 us -> 809 us (1.41)
  waiting for transfers between devices: 260 us -> 455 us
  other arithmetic: 39.9 us -> 61 us
  starting transfers between devices: 45.6 us -> 55 us
    all_gather x0 -> x1, waiting for transfers between devices: none -> 244 us  [body(): lax.all_gather(far_grads[:NGLOBAL * BLOCK], ('row', 'col'))]
    psum x1 -> x0, waiting for transfers between devices: 64.7 us -> none  [body(): global_sum = lax.psum(far_grads[:NGLOBAL * BLOCK], ('row', 'col'))]
    ppermute x2, waiting for transfers between devices: 48.1 us -> 84.5 us  [extended_2(): before = lax.ppermute(last, axis, up)]
    reduce_sum x0 -> x1, other arithmetic: none -> 22.3 us  [body(): jnp.sum(lax.all_gather(far_grads[:NGLOBAL * BLOCK], ('row', 'col')), axis=0)]
    all_to_all x2, waiting for transfers between devices: 53.5 us -> 35.6 us  [route_blocks(): lax.all_to_all(split_rows, 'col', split_axis=1, concat_axis=1, tiled=True)]
    all_to_all x2, starting transfers between devices: 22.9 us -> 31.9 us  [route_blocks(): lax.all_to_all(arranged, 'col', split_axis=1, concat_axis=1, tiled=True)]
    unnamed x249 -> x269, local copies, waits for them, and re-layouts: 35.2 us -> 42.5 us
  transfers between devices with their start and end apart: 10 -> 10, of which waited for: 6 -> 6; matrix products, arithmetic and copies ran while one was open for 11% -> 15% of each run, Pallas kernels for 0% -> 0%
where the time goes in v1:
time: 809 us; the launch traced here: 803 us
  waiting for transfers between devices  455 us (56%)
  local copies, waits for them, and re-layouts  139 us (17%)
  matrix products  69.7 us (9%)
  other arithmetic  61 us (8%)
  starting transfers between devices  55 us (7%)
  between operations  22.8 us (3%)
    all_gather x1, waiting for transfers between devices, body(): lax.all_gather(far_grads[:NGLOBAL * BLOCK], ('row', 'col'))  244 us
    psum x1, waiting for transfers between devices, spread(): return lax.psum(jnp.where(mine, value, jnp.zeros_like(value)), axis)  90.8 us
    ppermute x2, waiting for transfers between devices, extended_2(): before = lax.ppermute(last, axis, up)  84.5 us
    unnamed x269, local copies, waits for them, and re-layouts  42.5 us
    all_to_all x2, waiting for transfers between devices, route_blocks(): lax.all_to_all(split_rows, 'col', split_axis=1, concat_axis=1, tiled=True)  35.6 us
    all_to_all x2, starting transfers between devices, route_blocks(): lax.all_to_all(arranged, 'col', split_axis=1, concat_axis=1, tiled=True)  31.9 us
    slice x19, local copies, waits for them, and re-layouts, split_heads(): part_cols = array[..., lower:upper]  26.4 us
    reduce_sum x1, other arithmetic, body(): jnp.sum(lax.all_gather(far_grads[:NGLOBAL * BLOCK], ('row', 'col')), axis=0)  22.3 us
  transfers between devices with their start and end apart: 10, of which 6 were waited for; matrix products, arithmetic and copies ran while one was open for 15% of the time, Pallas kernels for 0%

profile of v1, /device:TPU:0, one launch (start us, length us, event | category | flops | bytes accessed | tf_op | source)
XLA Modules:
  0.0 802.5 jit_solution(8017639387991613444)
XLA Ops:
  22.8 7.5 all-to-all-start
  31.0 31.2 %all-to-all-done = bf16[3,16,8,2048]{3,2,0,1:T(8,128)(2,1)S(1)} async-done(((bf16[3,16,8,2048]{3,2,0,1:T(8,128)(2,1)}), bf16[3,16,8,2048]{3,2,0,1:T(8,128)(2,1)S(1)}, u32[]{:S(2)}, u32[]{:S(2)}) %all-to-all-start) | async-done | bytes 1572896 | tf_op jit(solution)/shard_map/all_to_all | solution.py:50
  68.6 9.3 %all-to-all-start.1 = ((bf16[3,16,8,2048]{3,2,0,1:T(8,128)(2,1)}), bf16[3,16,8,2048]{3,2,0,1:T(8,128)(2,1)}, u32[]{:S(2)}, u32[]{:S(2)}) async-start(bf16[3,16,8,2048]{3,2,0,1:T(8,128)(2,1)} %copy.632), calls=%async_computation.1 | async-start | bytes 3145728 | tf_op jit(solution)/shard_map/all_to_all | solution.py:52
  78.4 5.0 collective-permute-start.1
  84.3 3.8 convert_multiply_fusion
  96.6 22.9 %collective-permute-done = bf16[128,2048]{1,0:T(8,128)(2,1)} collective-permute-done((bf16[128,2048]{1,0:T(8,128)(2,1)}, bf16[128,2048]{1,0:T(8,128)(2,1)}, u32[]{:S(2)}, u32[]{:S(2)}) %collective-permute-start) | collective-permute-done | bytes 524320 | tf_op jit(solution)/shard_map/ppermute | solution.py:22
  136.1 2.7 copy.633
  138.9 90.8 %all-reduce.4.cloned.1.call-done = (bf16[128,2048]{1,0:T(8,128)(2,1)}, bf16[128,2048]{1,0:T(8,128)(2,1)}) async-done(((bf16[128,2048]{1,0:T(8,128)(2,1)}, bf16[128,2048]{1,0:T(8,128)(2,1)}), (bf16[128,2048]{1,0:T(8,128)(2,1)}, bf16[128,2048]{1,0:T(8,128)(2,1)})) %all-reduce.4.cloned.1.call-update) | async-done | bytes 1048592 | tf_op jit(solution)/shard_map/psum | solution.py:30
  271.0 5.1 multiply_reduce_fusion.3
  281.4 7.5 multiply_convert_fusion.3
  288.9 2.7 fusion.41
  305.2 2.7 fusion.44
  310.1 2.7 fusion.118
  315.0 2.7 fusion.114
  319.8 2.7 fusion.110
  324.6 2.7 fusion.106
  337.3 3.1 slice.404
  347.7 4.8 all-to-all-start.2
  404.8 4.3 all-to-all-done.2
  422.1 22.6 %all-to-all-start.3 = ((bf16[3,16,8,2048]{3,2,0,1:T(8,128)(2,1)}), bf16[3,16,8,2048]{3,2,0,1:T(8,128)(2,1)}, u32[]{:S(2)}, u32[]{:S(2)}) async-start(bf16[3,16,8,2048]{3,2,0,1:T(8,128)(2,1)} %copy.758), calls=%async_computation.3 | async-start | bytes 3145728 | tf_op jit(solution)/shard_map/all_to_all | solution.py:52
  450.0 5.0 collective-permute-start.3
  457.3 61.6 %collective-permute-done.2 = bf16[128,2048]{1,0:T(8,128)(2,1)} collective-permute-done((bf16[128,2048]{1,0:T(8,128)(2,1)}, bf16[128,2048]{1,0:T(8,128)(2,1)}, u32[]{:S(2)}, u32[]{:S(2)}) %collective-permute-start.2) | collective-permute-done | bytes 524320 | tf_op jit(solution)/shard_map/ppermute | solution.py:22
  521.7 244.4 %all-gather.3.cloned.1.call-done = f32[8192,2048]{1,0:T(8,128)} async-done(((f32[256,2048]{1,0:T(8,128)}), f32[8192,2048]{1,0:T(8,128)}) %all-gather.3.cloned.1.call-update) | async-done | bytes 67108880 | tf_op jit(solution)/shard_map/all_gather | solution.py:208
  766.1 22.3 %reduce_sum.179 = f32[256,2048]{1,0:T(8,128)} reduce(f32[32,256,2048]{2,1,0:T(8,128)} %bitcast.158, f32[]{:T(128)} %constant.196.clone.1), dimensions={0}, to_apply=%region_27.28 | reduce | flops 16252928 | bytes 69206016 | tf_op jit(solution)/shard_map/reduce_sum | solution.py:208
  (465 shorter events, 209.6 us)
Async XLA Ops:
  7.2 12.7 %copy-start.91 = (bf16[256,1024]{1,0:T(8,128)(2,1)S(1)}, bf16[256,1024]{1,0:T(8,128)(2,1)}, u32[]{:S(2)}) copy-start(bf16[256,1024]{1,0:T(8,128)(2,1)} %param.18) | copy-start | bytes 1572868
  22.8 39.4 %all-to-all-start = ((bf16[3,16,8,2048]{3,2,0,1:T(8,128)(2,1)}), bf16[3,16,8,2048]{3,2,0,1:T(8,128)(2,1)S(1)}, u32[]{:S(2)}, u32[]{:S(2)}) async-start(bf16[3,16,8,2048]{3,2,0,1:T(8,128)(2,1)} %pad_maximum_fusion.1), calls=%async_computation | async-start | bytes 3145728 | tf_op jit(solution)/shard_map/all_to_all | solution.py:50
  68.6 14.8 %copy-start.100 = (s32[256,128]{1,0:T(8,128)S(1)}, s32[256,128]{1,0:T(8,128)}, u32[]{:S(2)}) copy-start(s32[256,128]{1,0:T(8,128)} %param.20) | copy-start | bytes 393220
  68.6 67.5 %all-to-all-start.1 = ((bf16[3,16,8,2048]{3,2,0,1:T(8,128)(2,1)}), bf16[3,16,8,2048]{3,2,0,1:T(8,128)(2,1)}, u32[]{:S(2)}, u32[]{:S(2)}) async-start(bf16[3,16,8,2048]{3,2,0,1:T(8,128)(2,1)} %copy.632), calls=%async_computation.1 | async-start | bytes 3145728 | tf_op jit(solution)/shard_map/all_to_all | solution.py:52
  77.9 151.8 %all-reduce.4.cloned.1.call-start = ((), (), s32[]{:S(2)}) async-start(), calls=%async_computation.5 | async-start | bytes 2097152 | tf_op jit(solution)/shard_map/psum | solution.py:30
  77.9 41.5 %collective-permute-start = (bf16[128,2048]{1,0:T(8,128)(2,1)}, bf16[128,2048]{1,0:T(8,128)(2,1)}, u32[]{:S(2)}, u32[]{:S(2)}) collective-permute-start(bf16[128,2048]{1,0:T(8,128)(2,1)} %get-tuple-element.112), channel_id=1, source_target_pairs={{0,1},{1,2},{2,3},{3,4},{4,5},{5,6},{6,7},{7,8},{8,9},{9,10},{10,1... | collective-permute-start | bytes 1572872 | tf_op jit(solution)/shard_map/ppermute | solution.py:22
  78.4 41.1 %collective-permute-start.1 = (bf16[128,2048]{1,0:T(8,128)(2,1)}, bf16[128,2048]{1,0:T(8,128)(2,1)}, u32[]{:S(2)}, u32[]{:S(2)}) collective-permute-start(bf16[128,2048]{1,0:T(8,128)(2,1)} %get-tuple-element.118), channel_id=1, source_target_pairs={{1,0},{2,1},{3,2},{4,3},{5,4},{6,5},{7,6},{8,7},{9,8},{10,9},{11,1... | collective-permute-start | bytes 1572872 | tf_op jit(solution)/shard_map/ppermute | solution.py:23
  83.4 682.7 %all-gather.3.cloned.1.call-start = ((), (), s32[]{:S(2)}) async-start(), calls=%async_computation.4 | async-start | bytes 69206016 | tf_op jit(solution)/shard_map/all_gather | solution.py:208
  89.7 41.2 %copy-start.59 = (bf16[2,128,256]{1,2,0:T(8,128)(2,1)}, bf16[2,128,256]{1,2,0:T(8,128)(2,1)S(1)}, u32[]{:S(2)}) copy-start(bf16[2,128,256]{1,2,0:T(8,128)(2,1)S(1)} %copy.819) | copy-start | bytes 393220
  92.8 39.7 %copy-start.61 = (bf16[2,128,256]{1,2,0:T(8,128)(2,1)}, bf16[2,128,256]{1,2,0:T(8,128)(2,1)S(1)}, u32[]{:S(2)}) copy-start(bf16[2,128,256]{1,2,0:T(8,128)(2,1)S(1)} %copy.825) | copy-start | bytes 393220
  122.7 9.7 %copy-start.37 = (bf16[2,384,256]{1,2,0:T(8,128)(2,1)}, bf16[2,384,256]{1,2,0:T(8,128)(2,1)S(1)}, u32[]{:S(2)}) copy-start(bf16[2,384,256]{1,2,0:T(8,128)(2,1)S(1)} %copy.648) | copy-start | bytes 1179652
  124.1 10.0 %copy-start.39 = (bf16[2,384,256]{1,2,0:T(8,128)(2,1)}, bf16[2,384,256]{1,2,0:T(8,128)(2,1)S(1)}, u32[]{:S(2)}) copy-start(bf16[2,384,256]{1,2,0:T(8,128)(2,1)S(1)} %copy.661) | copy-start | bytes 1179652
  347.7 61.5 %all-to-all-start.2 = ((bf16[3,16,8,2048]{3,2,0,1:T(8,128)(2,1)}), bf16[3,16,8,2048]{3,2,0,1:T(8,128)(2,1)}, u32[]{:S(2)}, u32[]{:S(2)}) async-start(bf16[3,16,8,2048]{3,2,0,1:T(8,128)(2,1)} %copy.754), calls=%async_computation.2 | async-start | bytes 3145728 | tf_op jit(solution)/shard_map/all_to_all | solution.py:50
  404.8 41.6 %copy-start.16 = (f32[384,2048]{1,0:T(8,128)}, f32[384,2048]{1,0:T(8,128)S(1)}, u32[]{:S(2)}) copy-start(f32[384,2048]{1,0:T(8,128)S(1)} %fusion) | copy-start | bytes 9437188
  422.1 22.6 %copy-start.36 = (bf16[2,384,256]{1,2,0:T(8,128)(2,1)S(1)}, bf16[2,384,256]{1,2,0:T(8,128)(2,1)}, u32[]{:S(2)}) copy-start(bf16[2,384,256]{1,2,0:T(8,128)(2,1)} %copy-done.35) | copy-start | bytes 1179652
  422.1 368.4 %all-to-all-start.3 = ((bf16[3,16,8,2048]{3,2,0,1:T(8,128)(2,1)}), bf16[3,16,8,2048]{3,2,0,1:T(8,128)(2,1)}, u32[]{:S(2)}, u32[]{:S(2)}) async-start(bf16[3,16,8,2048]{3,2,0,1:T(8,128)(2,1)} %copy.758), calls=%async_computation.3 | async-start | bytes 3145728 | tf_op jit(solution)/shard_map/all_to_all | solution.py:52
  446.2 8.7 %copy-start.93 = (bf16[32,8,2,128]{3,1,2,0:T(8,128)(2,1)S(1)}, bf16[32,8,2,128]{3,1,2,0:T(8,128)(2,1)}, u32[]{:S(2)}) copy-start(bf16[32,8,2,128]{3,1,2,0:T(8,128)(2,1)} %copy.959) | copy-start | bytes 393220
  446.2 8.7 %copy-start.94 = (bf16[32,8,2,128]{3,1,2,0:T(8,128)(2,1)S(1)}, bf16[32,8,2,128]{3,1,2,0:T(8,128)(2,1)}, u32[]{:S(2)}) copy-start(bf16[32,8,2,128]{3,1,2,0:T(8,128)(2,1)} %copy.960) | copy-start | bytes 393220
  446.2 8.7 %copy-start.95 = (bf16[32,8,2,128]{3,1,2,0:T(8,128)(2,1)S(1)}, bf16[32,8,2,128]{3,1,2,0:T(8,128)(2,1)}, u32[]{:S(2)}) copy-start(bf16[32,8,2,128]{3,1,2,0:T(8,128)(2,1)} %copy.961) | copy-start | bytes 393220
  446.2 8.7 %copy-start.96 = (bf16[32,8,2,128]{3,1,2,0:T(8,128)(2,1)S(1)}, bf16[32,8,2,128]{3,1,2,0:T(8,128)(2,1)}, u32[]{:S(2)}) copy-start(bf16[32,8,2,128]{3,1,2,0:T(8,128)(2,1)} %copy.962) | copy-start | bytes 393220
  446.4 8.5 %copy-start.97 = (bf16[32,8,2,128]{3,1,2,0:T(8,128)(2,1)S(1)}, bf16[32,8,2,128]{3,1,2,0:T(8,128)(2,1)}, u32[]{:S(2)}) copy-start(bf16[32,8,2,128]{3,1,2,0:T(8,128)(2,1)} %copy.955) | copy-start | bytes 393220
  446.4 8.5 %copy-start.98 = (bf16[32,8,2,128]{3,1,2,0:T(8,128)(2,1)S(1)}, bf16[32,8,2,128]{3,1,2,0:T(8,128)(2,1)}, u32[]{:S(2)}) copy-start(bf16[32,8,2,128]{3,1,2,0:T(8,128)(2,1)} %copy.956) | copy-start | bytes 393220
  447.3 71.6 %collective-permute-start.2 = (bf16[128,2048]{1,0:T(8,128)(2,1)}, bf16[128,2048]{1,0:T(8,128)(2,1)}, u32[]{:S(2)}, u32[]{:S(2)}) collective-permute-start(bf16[128,2048]{1,0:T(8,128)(2,1)} %slice.505), channel_id=1, source_target_pairs={{0,1},{1,2},{2,3},{3,4},{4,5},{5,6},{6,7},{7,8},{8,9},{9,10},{10,1... | collective-permute-start | bytes 1572872 | tf_op jit(solution)/shard_map/ppermute | solution.py:22
  450.0 70.5 %collective-permute-start.3 = (bf16[128,2048]{1,0:T(8,128)(2,1)}, bf16[128,2048]{1,0:T(8,128)(2,1)}, u32[]{:S(2)}, u32[]{:S(2)}) collective-permute-start(bf16[128,2048]{1,0:T(8,128)(2,1)} %fusion.98), channel_id=1, source_target_pairs={{1,0},{2,1},{3,2},{4,3},{5,4},{6,5},{7,6},{8,7},{9,8},{10,9},{11,1... | collective-permute-start | bytes 1572872 | tf_op jit(solution)/shard_map/ppermute | solution.py:23
  (102 other events, 241.5 us)
Sparse Core Ops, SparseCore 0:
  84.7 144.9 all-reduce.3
  340.6 425.4 all-gather.2
